TPU v7x, 512 devices: a whole 4x8x8 slice. The times are simulated.
512 devices in a mesh: dp: 32 (over y_lo, z), row: 4 (over x), col: 4 (over y_hi, core).
Axes of the slice: x: 4, y: 8 (y_hi: 2, y_lo: 4; y = y_hi * 4 + y_lo), z: 8, core: 2. Of those that a mesh axis runs over, the one named last changes fastest.
Arguments:
- query_out: bfloat16 [6144, 4096], P(('dp', 'row'), 'col'), may hold values from -6 to 6
- query_in: bfloat16 [6144, 4096], P(('dp', 'col')), may hold values from -6 to 6
- out_basis: bfloat16 [4096, 4096], P('col', ('dp', 'row')), may hold values from -0.09375 to 0.09375
- in_basis: bfloat16 [4096, 4096], P(('dp', 'row'), 'col'), may hold values from -0.09375 to 0.09375
- eigvals: float32 [4096, 4096], P(('dp', 'row'), 'col'), may hold values from 16 to 1024
- train_out: bfloat16 [6144, 4096], P(('dp', 'row'), 'col'), may hold values from -0.09375 to 0.09375
- train_in: bfloat16 [6144, 4096], P(('dp', 'col')), may hold values from -0.09375 to 0.09375
Outputs:
- precond: float32 [4096, 4096], P(('dp', 'row'), 'col')
- scores: float32 [6144], P('dp')
All inputs are finite; a program needn't handle non-finite values.
Results may differ from a plain program's by a relative error of at most 0.028.
Values may be sent and summed in bfloat16 or wider, within the bound.
No kernel may reach another device: no remote copies, remote signals or barrier semaphores. Data moves between devices by JAX's collectives and lax.ppermute only.
A program may use at most 64 MiB of HBM per device.

v0:
```python
import jax
import jax.numpy as jnp
from jax import lax
from jax.sharding import PartitionSpec as P

damping = 1.0


def rotate_out(tok_rows, basis_panel):
    gathered = lax.all_gather(tok_rows, "row", axis=0, tiled=True)
    partial_sum = jnp.dot(gathered, basis_panel, preferred_element_type=jnp.float32)
    return lax.psum(partial_sum.astype(jnp.bfloat16), "col")


def rotate_in(tok_rows, basis_panel):
    groups = lax.axis_size("dp")
    row_count = lax.axis_size("row")
    sub_width = tok_rows.shape[1] // (groups * row_count)
    split_rows = tok_rows.reshape(tok_rows.shape[0], groups, row_count, sub_width)
    picked = lax.dynamic_index_in_dim(split_rows, lax.axis_index("row"), 2, keepdims=False)
    picked = picked.reshape(tok_rows.shape[0], groups * sub_width)
    gathered = lax.all_gather(picked, "col", axis=0, tiled=True)
    partial_sum = jnp.dot(gathered, basis_panel, preferred_element_type=jnp.float32)
    return lax.psum(partial_sum.astype(jnp.bfloat16), "row")


def per_device(query_out, query_in, out_basis, in_basis, eigvals, train_out, train_in):
    panel_out = lax.all_gather(out_basis, "dp", axis=1, tiled=True)
    panel_in = lax.all_gather(in_basis, "dp", axis=0, tiled=True)
    query_rot = rotate_out(query_out, panel_out)
    query_inr = rotate_in(query_in, panel_in)
    partial_grad = lax.dot_general(
        query_rot, query_inr, (((0,), (0,)), ((), ())), preferred_element_type=jnp.float32
    )
    rows_own = eigvals.shape[0]
    summed = lax.psum(partial_grad.astype(jnp.bfloat16), "dp").astype(jnp.float32)
    owned = lax.dynamic_slice_in_dim(summed, lax.axis_index("dp") * rows_own, rows_own, 0)
    precond = owned / (eigvals + damping)
    shared = precond.astype(jnp.bfloat16)
    train_rot = rotate_out(train_out, panel_out)
    train_inr = rotate_in(train_in, panel_in)
    mixed = jnp.dot(
        train_rot,
        lax.all_gather(shared, "dp", axis=0, tiled=True),
        preferred_element_type=jnp.float32,
    )
    partial_scores = jnp.sum(mixed * train_inr.astype(jnp.float32), axis=1)
    scores = lax.psum(partial_scores, ("row", "col"))
    return (precond, scores)


def solution(mesh):
    in_specs = (
        P(("dp", "row"), "col"),
        P(("dp", "col"), None),
        P("col", ("dp", "row")),
        P(("dp", "row"), "col"),
        P(("dp", "row"), "col"),
        P(("dp", "row"), "col"),
        P(("dp", "col"), None),
    )
    out_specs = (P(("dp", "row"), "col"), P("dp"))
    return jax.shard_map(
        per_device, mesh=mesh, in_specs=in_specs, out_specs=out_specs, check_vma=False
    )
```

profile of v0, /device:TPU:1, one launch (start us, length us, event | category | flops | bytes accessed | tf_op | source)
XLA Modules:
  0.0 969.9 jit_solution(9535577205798143316)
XLA Ops:
  7.2 0.0 all-gather.6.cloned.1.call-start
  7.2 0.7 all-gather.6.cloned.1.call-update
  7.9 0.0 all-gather.4.cloned.1.call-start
  7.9 0.7 all-gather.4.cloned.1.call-update
  8.6 0.0 all-reduce.10.cloned.1.call-start
  8.7 1.5 copy.9
  10.2 1.5 copy.11
  11.7 0.1 copy.14
  11.8 0.1 copy.13
  12.0 16.7 %all_gather.27 = bf16[192,1024]{1,0:T(8,128)(2,1)S(1)} all-gather(bf16[48,1024]{1,0:T(8,128)(2,1)S(1)} %copy.14), channel_id=1, replica_groups=mesh['dp'=32,'row'=4,'col'=4] {'col'}, dimensions={0}, use_global_device_ids=true | all-gather | bytes 491520 | tf_op jit(solution)/shard_map/all_gather | solution.py:22
  28.7 12.9 %all_gather.23 = bf16[192,1024]{1,0:T(8,128)(2,1)S(1)} all-gather(bf16[48,1024]{1,0:T(8,128)(2,1)S(1)} %copy.13), channel_id=1, replica_groups=mesh['dp'=32,'row'=4,'col'=4] {'col'}, dimensions={0}, use_global_device_ids=true | all-gather | bytes 491520 | tf_op jit(solution)/shard_map/all_gather | solution.py:22
  41.6 106.6 %all-gather.6.cloned.1.call-done = bf16[1024,1024]{1,0:T(8,128)(2,1)} async-done(((bf16[32,1024]{1,0:T(8,128)(2,1)}), bf16[1024,1024]{1,0:T(8,128)(2,1)}) %all-gather.6.cloned.1.call-update) | async-done | bytes 2097168 | tf_op jit(solution)/shard_map/all_gather | solution.py:29
  148.2 0.0 copy-start.1
  148.2 3.1 convolution_convert_fusion.1
  151.3 0.0 copy-done.1
  151.3 0.0 copy-start.3
  151.3 0.0 copy-start.4
  151.3 1.4 convolution_convert_fusion.3
  152.7 0.0 all-reduce.10.cloned.1.call-update
  152.7 0.0 all-reduce.8.cloned.1.call-start
  152.8 0.0 copy-done.3
  152.8 10.9 %all_gather.25 = bf16[192,1024]{1,0:T(8,128)(2,1)S(1)} all-gather(bf16[48,1024]{1,0:T(8,128)(2,1)S(1)} %copy-done.3), channel_id=1, replica_groups=mesh['dp'=32,'row'=4,'col'=4] {'row'}, dimensions={0}, use_global_device_ids=true | all-gather | bytes 491520 | tf_op jit(solution)/shard_map/all_gather | solution.py:10
  163.6 0.0 copy-done.4
  163.6 10.0 %all_gather.21 = bf16[192,1024]{1,0:T(8,128)(2,1)S(1)} all-gather(bf16[48,1024]{1,0:T(8,128)(2,1)S(1)} %copy-done.4), channel_id=1, replica_groups=mesh['dp'=32,'row'=4,'col'=4] {'row'}, dimensions={0}, use_global_device_ids=true | all-gather | bytes 491520 | tf_op jit(solution)/shard_map/all_gather | solution.py:10
  173.6 126.9 %all-gather.4.cloned.1.call-done = bf16[1024,1024]{0,1:T(8,128)(2,1)} async-done(((bf16[1024,32]{0,1:T(8,128)(2,1)}), bf16[1024,1024]{0,1:T(8,128)(2,1)}) %all-gather.4.cloned.1.call-update) | async-done | bytes 2097168 | tf_op jit(solution)/shard_map/all_gather | solution.py:28
  300.6 0.0 copy-start
  300.6 3.3 convolution_convert_fusion.2
  303.9 0.0 copy-done
  303.9 1.6 convolution_convert_fusion.4
  305.5 0.0 all-reduce.8.cloned.1.call-update
  305.5 0.0 all-reduce.6.cloned.1.call-start
  305.6 68.1 %all-reduce.10.cloned.1.call-done = (bf16[192,1024]{1,0:T(8,128)(2,1)}, bf16[192,1024]{1,0:T(8,128)(2,1)}) async-done(((bf16[192,1024]{1,0:T(8,128)(2,1)}, bf16[192,1024]{1,0:T(8,128)(2,1)}), (bf16[192,1024]{1,0:T(8,128)(2,1)}, bf16[192,1024]{1,0:T(8,128)(2,1)})) %all-reduce.10.cloned.1.call-update) | async-done | bytes 786448 | tf_op jit(solution)/shard_map/psum | solution.py:24
  373.7 75.0 %all-reduce.8.cloned.1.call-done = (bf16[192,1024]{1,0:T(8,128)(2,1)}, bf16[192,1024]{1,0:T(8,128)(2,1)}) async-done(((bf16[192,1024]{1,0:T(8,128)(2,1)}, bf16[192,1024]{1,0:T(8,128)(2,1)}), (bf16[192,1024]{1,0:T(8,128)(2,1)}, bf16[192,1024]{1,0:T(8,128)(2,1)})) %all-reduce.8.cloned.1.call-update) | async-done | bytes 786448 | tf_op jit(solution)/shard_map/psum | solution.py:12
  448.7 0.0 copy-start.2
  448.7 0.0 copy-start.5
  448.7 0.0 copy-start.6
  448.7 3.3 convolution_convert_fusion
  451.9 0.0 all-reduce.6.cloned.1.call-update
  452.0 0.0 all-gather.8.cloned.1.call-start
  452.0 290.8 %all-reduce.6.cloned.1.call-done = bf16[1024,1024]{1,0:T(8,128)(2,1)} async-done(((bf16[1024,1024]{1,0:T(8,128)(2,1)}), bf16[1024,1024]{1,0:T(8,128)(2,1)}) %all-reduce.6.cloned.1.call-update) | async-done | bytes 2097168 | tf_op jit(solution)/shard_map/psum | solution.py:36
  742.8 0.0 copy-done.2
  742.8 1.5 fusion.1
  744.3 0.0 all-gather.8.cloned.1.call-update
  744.4 150.6 %all-gather.8.cloned.1.call-done = bf16[1024,1024]{1,0:T(8,128)(2,1)} async-done(((bf16[32,1024]{1,0:T(8,128)(2,1)}), bf16[1024,1024]{1,0:T(8,128)(2,1)}) %all-gather.8.cloned.1.call-update) | async-done | bytes 2097168 | tf_op jit(solution)/shard_map/all_gather | solution.py:44
  895.0 0.0 copy-done.5
  895.0 0.0 copy-done.6
  895.0 2.3 fusion
  897.2 65.8 %psum.47 = f32[192]{0:T(256)} all-reduce(f32[192]{0:T(256)S(1)} %fusion), channel_id=1, replica_groups=mesh['dp'=32,'row'=4,'col'=4] {'row','col'}, use_global_device_ids=true, to_apply=%region_6.7 | all-reduce | flops 192 | bytes 1536 | tf_op jit(solution)/shard_map/psum | solution.py:48
  (1 shorter events, 0.0 us)
Async XLA Ops:
  7.2 141.1 %all-gather.6.cloned.1.call-start = ((), (), s32[]{:S(2)}) async-start(), calls=%async_computation.1 | async-start | bytes 2162688 | tf_op jit(solution)/shard_map/all_gather | solution.py:29
  7.9 292.7 %all-gather.4.cloned.1.call-start = ((), (), s32[]{:S(2)}) async-start(), calls=%async_computation | async-start | bytes 2162688 | tf_op jit(solution)/shard_map/all_gather | solution.py:28
  8.6 365.1 %all-reduce.10.cloned.1.call-start = ((), (), s32[]{:S(2)}) async-start(), calls=%async_computation.5 | async-start | bytes 1572864 | tf_op jit(solution)/shard_map/psum | solution.py:24
  148.2 3.1 copy-start.1
  151.3 1.4 copy-start.3
  151.3 12.3 %copy-start.4 = (bf16[48,1024]{1,0:T(8,128)(2,1)S(1)}, bf16[48,1024]{1,0:T(8,128)(2,1)}, u32[]{:S(2)}) copy-start(bf16[48,1024]{1,0:T(8,128)(2,1)} %param.7) | copy-start | bytes 294916
  152.7 295.9 %all-reduce.8.cloned.1.call-start = ((), (), s32[]{:S(2)}) async-start(), calls=%async_computation.4 | async-start | bytes 1572864 | tf_op jit(solution)/shard_map/psum | solution.py:12
  300.6 3.3 copy-start
  305.5 437.3 %all-reduce.6.cloned.1.call-start = ((), (), s32[]{:S(2)}) async-start(), calls=%async_computation.2 | async-start | bytes 4194304 | tf_op jit(solution)/shard_map/psum | solution.py:36
  448.7 294.2 %copy-start.2 = (f32[32,1024]{1,0:T(8,128)S(1)}, f32[32,1024]{1,0:T(8,128)}, u32[]{:S(2)}) copy-start(f32[32,1024]{1,0:T(8,128)} %param.11) | copy-start | bytes 393220
  448.7 446.3 %copy-start.5 = (bf16[192,1024]{1,0:T(8,128)(2,1)S(1)}, bf16[192,1024]{1,0:T(8,128)(2,1)}, u32[]{:S(2)}) copy-start(bf16[192,1024]{1,0:T(8,128)(2,1)} %get-tuple-element.5) | copy-start | bytes 1179652
  448.7 446.3 %copy-start.6 = (bf16[192,1024]{1,0:T(8,128)(2,1)S(1)}, bf16[192,1024]{1,0:T(8,128)(2,1)}, u32[]{:S(2)}) copy-start(bf16[192,1024]{1,0:T(8,128)(2,1)} %get-tuple-element.3) | copy-start | bytes 1179652
  452.0 443.0 %all-gather.8.cloned.1.call-start = ((), (), s32[]{:S(2)}) async-start(), calls=%async_computation.3 | async-start | bytes 2162688 | tf_op jit(solution)/shard_map/all_gather | solution.py:44
Sparse Core Ops, SparseCore 0:
  10.0 138.1 all-gather.5
  150.3 150.2 all-gather.3
  303.0 70.6 all-reduce.9
  376.6 72.0 all-reduce.7
  452.1 290.6 all-reduce.5
  744.7 150.1 all-gather.7
where the time goes:
time: 970 us
  waiting for transfers between devices  819 us (84%)
  blocking collectives  116 us (12%)
  matrix products  14.9 us (2%)
  between operations  14.2 us (1%)
    psum x1, waiting for transfers between devices, per_device(): lax.psum(partial_grad.astype(jnp.bfloat16), 'dp').astype(jnp.float32)  291 us
    all_gather x1, waiting for transfers between devices, per_device(): lax.all_gather(shared, 'dp', axis=0, tiled=True)  151 us
    all_gather x1, waiting for transfers between devices, per_device(): panel_out = lax.all_gather(out_basis, 'dp', axis=1, tiled=True)  127 us
    all_gather x1, waiting for transfers between devices, per_device(): panel_in = lax.all_gather(in_basis, 'dp', axis=0, tiled=True)  107 us
    psum x1, waiting for transfers between devices, rotate_out(): return lax.psum(partial_sum.astype(jnp.bfloat16), 'col')  75 us
    psum x1, waiting for transfers between devices, rotate_in(): return lax.psum(partial_sum.astype(jnp.bfloat16), 'row')  68.1 us
    psum x1, blocking collectives, per_device(): scores = lax.psum(partial_scores, ('row', 'col'))  65.8 us
    all_gather x2, blocking collectives, rotate_in(): gathered = lax.all_gather(picked, 'col', axis=0, tiled=True)  29.6 us
  transfers between devices with their start and end apart: 6, of which 6 were waited for; matrix products, arithmetic and copies ran while one was open for 1% of the time, Pallas kernels for 0%

commit v1 on v0

--- a/solution.py
+++ b/solution.py
@@ -41,7 +41,9 @@
     train_inr = rotate_in(train_in, panel_in)
     mixed = jnp.dot(
         train_rot,
-        lax.all_gather(shared, "dp", axis=0, tiled=True),
+        jnp.concatenate(
+            lax.all_to_all(jnp.stack([shared] * lax.axis_size("dp")), "dp", 0, 0), axis=0
+        ),
         preferred_element_type=jnp.float32,
     )
     partial_scores = jnp.sum(mixed * train_inr.astype(jnp.float32), axis=1)

time: 970 us -> 863 us (0.89)
  waiting for transfers between devices: 819 us -> 654 us
  blocking collectives: 116 us -> 177 us
    all_gather x1 -> x0, waiting for transfers between devices: 151 us -> none  [per_device(): lax.all_gather(shared, 'dp', axis=0, tiled=True)]
    all_to_all x0 -> x1, blocking collectives: none -> 33.7 us  [per_device(): lax.all_to_all(jnp.stack([shared] * lax.axis_size('dp')), 'dp', 0, 0)]
    all_gather x2, blocking collectives: 29.6 us -> 44.7 us  [rotate_in(): gathered = lax.all_gather(picked, 'col', axis=0, tiled=True)]
    psum x1, waiting for transfers between devices: 68.1 us -> 53.7 us  [rotate_in(): return lax.psum(partial_sum.astype(jnp.bfloat16), 'row')]
    psum x1, blocking collectives: 65.8 us -> 77.7 us  [per_device(): scores = lax.psum(partial_scores, ('row', 'col'))]
    all_gather x1, waiting for transfers between devices: 127 us -> 116 us  [per_device(): panel_out = lax.all_gather(out_basis, 'dp', axis=1, tiled=True)]
    psum x1, waiting for transfers between devices: 75 us -> 85.3 us  [rotate_out(): return lax.psum(partial_sum.astype(jnp.bfloat16), 'col')]
  transfers between devices with their start and end apart: 6 -> 5, of which waited for: 6 -> 5; matrix products, arithmetic and copies ran while one was open for 1% -> 1% of each run, Pallas kernels for 0% -> 0%
where the time goes in v1:
time: 863 us
  waiting for transfers between devices  654 us (76%)
  blocking collectives  177 us (21%)
  between operations  13.9 us (2%)
  matrix products  13.3 us (2%)
    psum x1, waiting for transfers between devices, per_device(): lax.psum(partial_grad.astype(jnp.bfloat16), 'dp').astype(jnp.float32)  295 us
    all_gather x1, waiting for transfers between devices, per_device(): panel_out = lax.all_gather(out_basis, 'dp', axis=1, tiled=True)  116 us
    all_gather x1, waiting for transfers between devices, per_device(): panel_in = lax.all_gather(in_basis, 'dp', axis=0, tiled=True)  102 us
    psum x1, waiting for transfers between devices, rotate_out(): return lax.psum(partial_sum.astype(jnp.bfloat16), 'col')  85.3 us
    psum x1, blocking collectives, per_device(): scores = lax.psum(partial_scores, ('row', 'col'))  77.7 us
    psum x1, waiting for transfers between devices, rotate_in(): return lax.psum(partial_sum.astype(jnp.bfloat16), 'row')  53.7 us
    all_gather x2, blocking collectives, rotate_in(): gathered = lax.all_gather(picked, 'col', axis=0, tiled=True)  44.7 us
    all_to_all x1, blocking collectives, per_device(): lax.all_to_all(jnp.stack([shared] * lax.axis_size('dp')), 'dp', 0, 0)  33.7 us
  transfers between devices with their start and end apart: 5, of which 5 were waited for; matrix products, arithmetic and copies ran while one was open for 1% of the time, Pallas kernels for 0%

profile of v1, /device:TPU:1, one launch (start us, length us, event | category | flops | bytes accessed | tf_op | source)
XLA Modules:
  0.0 863.0 jit_solution(17560882267786839714)
XLA Ops:
  7.2 0.0 all-gather.3.cloned.1.call-start
  7.2 0.7 all-gather.3.cloned.1.call-update
  7.9 0.0 all-gather.5.cloned.1.call-start
  7.9 0.7 all-gather.5.cloned.1.call-update
  8.6 0.0 all-reduce.8.cloned.1.call-start
  8.7 0.0 copy-start.3
  8.7 0.0 copy-start.4
  8.7 1.5 copy.11
  10.2 1.5 copy.9
  11.8 0.1 copy.13
  11.9 0.0 copy-done.3
  11.9 10.8 %all_gather.18 = bf16[192,1024]{1,0:T(8,128)(2,1)S(1)} all-gather(bf16[48,1024]{1,0:T(8,128)(2,1)S(1)} %copy-done.3), channel_id=1, replica_groups=mesh['dp'=32,'row'=4,'col'=4] {'row'}, dimensions={0}, use_global_device_ids=true | all-gather | bytes 491520 | tf_op jit(solution)/shard_map/all_gather | solution.py:10
  22.7 0.0 copy-done.4
  22.7 9.6 %all_gather.22 = bf16[192,1024]{1,0:T(8,128)(2,1)S(1)} all-gather(bf16[48,1024]{1,0:T(8,128)(2,1)S(1)} %copy-done.4), channel_id=1, replica_groups=mesh['dp'=32,'row'=4,'col'=4] {'row'}, dimensions={0}, use_global_device_ids=true | all-gather | bytes 491520 | tf_op jit(solution)/shard_map/all_gather | solution.py:10
  32.3 115.9 %all-gather.3.cloned.1.call-done = bf16[1024,1024]{0,1:T(8,128)(2,1)} async-done(((bf16[1024,32]{0,1:T(8,128)(2,1)}), bf16[1024,1024]{0,1:T(8,128)(2,1)}) %all-gather.3.cloned.1.call-update) | async-done | bytes 2097168 | tf_op jit(solution)/shard_map/all_gather | solution.py:28
  148.3 0.0 copy-start.1
  148.3 3.3 convolution_convert_fusion.4
  151.6 0.0 copy-done.1
  151.6 1.6 convolution_convert_fusion.2
  153.2 0.0 all-reduce.8.cloned.1.call-update
  153.2 0.0 all-reduce.10.cloned.1.call-start
  153.3 33.9 %all_gather.20 = bf16[192,1024]{1,0:T(8,128)(2,1)S(1)} all-gather(bf16[48,1024]{1,0:T(8,128)(2,1)S(1)} %copy.13), channel_id=1, replica_groups=mesh['dp'=32,'row'=4,'col'=4] {'col'}, dimensions={0}, use_global_device_ids=true | all-gather | bytes 491520 | tf_op jit(solution)/shard_map/all_gather | solution.py:22
  187.2 0.1 copy.14
  187.3 10.8 %all_gather.23 = bf16[192,1024]{1,0:T(8,128)(2,1)S(1)} all-gather(bf16[48,1024]{1,0:T(8,128)(2,1)S(1)} %copy.14), channel_id=1, replica_groups=mesh['dp'=32,'row'=4,'col'=4] {'col'}, dimensions={0}, use_global_device_ids=true | all-gather | bytes 491520 | tf_op jit(solution)/shard_map/all_gather | solution.py:22
  198.1 102.2 %all-gather.5.cloned.1.call-done = bf16[1024,1024]{1,0:T(8,128)(2,1)} async-done(((bf16[32,1024]{1,0:T(8,128)(2,1)}), bf16[1024,1024]{1,0:T(8,128)(2,1)}) %all-gather.5.cloned.1.call-update) | async-done | bytes 2097168 | tf_op jit(solution)/shard_map/all_gather | solution.py:29
  300.4 0.0 copy-start
  300.4 3.1 convolution_convert_fusion.3
  303.4 0.0 copy-done
  303.4 1.3 convolution_convert_fusion.1
  304.8 0.0 all-reduce.10.cloned.1.call-update
  304.8 0.0 all-reduce.6.cloned.1.call-start
  304.9 85.3 %all-reduce.8.cloned.1.call-done = (bf16[192,1024]{1,0:T(8,128)(2,1)}, bf16[192,1024]{1,0:T(8,128)(2,1)}) async-done(((bf16[192,1024]{1,0:T(8,128)(2,1)}, bf16[192,1024]{1,0:T(8,128)(2,1)}), (bf16[192,1024]{1,0:T(8,128)(2,1)}, bf16[192,1024]{1,0:T(8,128)(2,1)})) %all-reduce.8.cloned.1.call-update) | async-done | bytes 786448 | tf_op jit(solution)/shard_map/psum | solution.py:12
  390.2 53.7 %all-reduce.10.cloned.1.call-done = (bf16[192,1024]{1,0:T(8,128)(2,1)}, bf16[192,1024]{1,0:T(8,128)(2,1)}) async-done(((bf16[192,1024]{1,0:T(8,128)(2,1)}, bf16[192,1024]{1,0:T(8,128)(2,1)}), (bf16[192,1024]{1,0:T(8,128)(2,1)}, bf16[192,1024]{1,0:T(8,128)(2,1)})) %all-reduce.10.cloned.1.call-update) | async-done | bytes 786448 | tf_op jit(solution)/shard_map/psum | solution.py:24
  443.9 0.0 copy-start.2
  443.9 3.2 convolution_convert_fusion
  447.2 0.0 all-reduce.6.cloned.1.call-update
  447.2 295.3 %all-reduce.6.cloned.1.call-done = bf16[1024,1024]{1,0:T(8,128)(2,1)} async-done(((bf16[1024,1024]{1,0:T(8,128)(2,1)}), bf16[1024,1024]{1,0:T(8,128)(2,1)}) %all-reduce.6.cloned.1.call-update) | async-done | bytes 2097168 | tf_op jit(solution)/shard_map/psum | solution.py:36
  742.5 0.0 copy-done.2
  742.5 1.5 fusion.1
  744.0 0.2 stack.2
  744.3 0.0 copy-start.5
  744.3 0.0 copy-start.6
  744.3 33.7 %all_to_all.5 = bf16[32,32,1024]{2,1,0:T(8,128)(2,1)S(1)} all-to-all(bf16[32,32,1024]{2,1,0:T(8,128)(2,1)S(1)} %stack.2), channel_id=1, replica_groups=mesh['dp'=32,'row'=4,'col'=4] {'dp'}, dimensions={0} | all-to-all | bytes 4194304 | tf_op jit(solution)/shard_map/all_to_all | solution.py:45
  778.1 0.0 copy-done.5
  778.1 0.0 copy-done.6
  778.1 0.7 fusion
  778.7 77.7 %psum.47 = f32[192]{0:T(256)} all-reduce(f32[192]{0:T(256)S(1)} %fusion), channel_id=1, replica_groups=mesh['dp'=32,'row'=4,'col'=4] {'row','col'}, use_global_device_ids=true, to_apply=%region_6.7 | all-reduce | flops 192 | bytes 1536 | tf_op jit(solution)/shard_map/psum | solution.py:50
  (1 shorter events, 0.0 us)
Async XLA Ops:
  7.2 141.1 %all-gather.3.cloned.1.call-start = ((), (), s32[]{:S(2)}) async-start(), calls=%async_computation.1 | async-start | bytes 2162688 | tf_op jit(solution)/shard_map/all_gather | solution.py:28
  7.9 292.5 %all-gather.5.cloned.1.call-start = ((), (), s32[]{:S(2)}) async-start(), calls=%async_computation.2 | async-start | bytes 2162688 | tf_op jit(solution)/shard_map/all_gather | solution.py:29
  8.6 381.6 %all-reduce.8.cloned.1.call-start = ((), (), s32[]{:S(2)}) async-start(), calls=%async_computation.4 | async-start | bytes 1572864 | tf_op jit(solution)/shard_map/psum | solution.py:12
  8.7 3.2 copy-start.3
  8.7 14.0 %copy-start.4 = (bf16[48,1024]{1,0:T(8,128)(2,1)S(1)}, bf16[48,1024]{1,0:T(8,128)(2,1)}, u32[]{:S(2)}) copy-start(bf16[48,1024]{1,0:T(8,128)(2,1)} %param.12) | copy-start | bytes 294916
  148.3 3.3 copy-start.1
  153.2 290.7 %all-reduce.10.cloned.1.call-start = ((), (), s32[]{:S(2)}) async-start(), calls=%async_computation.5 | async-start | bytes 1572864 | tf_op jit(solution)/shard_map/psum | solution.py:24
  300.4 3.1 copy-start
  304.8 437.7 %all-reduce.6.cloned.1.call-start = ((), (), s32[]{:S(2)}) async-start(), calls=%async_computation.3 | async-start | bytes 4194304 | tf_op jit(solution)/shard_map/psum | solution.py:36
  443.9 298.6 %copy-start.2 = (f32[32,1024]{1,0:T(8,128)S(1)}, f32[32,1024]{1,0:T(8,128)}, u32[]{:S(2)}) copy-start(f32[32,1024]{1,0:T(8,128)} %param.11) | copy-start | bytes 393220
  744.3 33.8 %copy-start.5 = (bf16[192,1024]{1,0:T(8,128)(2,1)S(1)}, bf16[192,1024]{1,0:T(8,128)(2,1)}, u32[]{:S(2)}) copy-start(bf16[192,1024]{1,0:T(8,128)(2,1)} %get-tuple-element.3) | copy-start | bytes 1179652
  744.3 33.8 %copy-start.6 = (bf16[192,1024]{1,0:T(8,128)(2,1)S(1)}, bf16[192,1024]{1,0:T(8,128)(2,1)}, u32[]{:S(2)}) copy-start(bf16[192,1024]{1,0:T(8,128)(2,1)} %get-tuple-element.5) | copy-start | bytes 1179652
Sparse Core Ops, SparseCore 0:
  10.1 138.1 all-gather.2
  150.3 149.9 all-gather.4
  303.4 86.7 all-reduce.7
  392.4 51.4 all-reduce.9
  447.3 295.1 all-reduce.5
